TPU v7x, 512 devices: a whole 4x8x8 slice. The times are simulated.
512 devices in a mesh: leaf: 8 (over z), row: 8 (over y), col: 8 (over x, core).
Axes of the slice: x: 4, y: 8, z: 8, core: 2. Of those that a mesh axis runs over, the one named last changes fastest.
Arguments:
- child_inverse: bfloat16 [8, 2, 3072, 3072], P('leaf', None, 'row', 'col'), as said below
- child_rhs: bfloat16 [8, 2, 3072, 256], P('leaf', None, 'col'), may hold values from -6 to 6
- child_to_mid: bfloat16 [8, 2, 2048, 3072], P('leaf', None, ('row', 'col')), may hold values from -0.109375 to 0.109375
- child_to_root: bfloat16 [8, 2, 2048, 3072], P('leaf', None, ('row', 'col')), may hold values from -0.109375 to 0.109375
- mid_rows_list: int32 [8, 2, 2048], P('leaf'), may hold values from 0 to 4095, as said below
- root_rows_list: int32 [8, 2, 2048], P('leaf'), may hold values from 0 to 8191, as said below
- mid_inverse: bfloat16 [8, 4096, 4096], P('leaf', 'row', 'col'), as said below
- mid_rhs: bfloat16 [8, 4096, 256], P('leaf', 'col'), may hold values from -6 to 6
- mid_to_root: bfloat16 [8, 2048, 4096], P('leaf', ('row', 'col')), may hold values from -0.09375 to 0.09375
- mid_root_list: int32 [8, 2048], P('leaf'), may hold values from 0 to 8191, as said below
- root_inverse: bfloat16 [8192, 8192], P(('leaf', 'row'), 'col'), as said below
- root_rhs: bfloat16 [8192, 256], P('col'), may hold values from -6 to 6
Outputs:
- child_solution: bfloat16 [8, 2, 3072, 256], P('leaf', None, 'row')
- mid_solution: bfloat16 [8, 4096, 256], P('leaf', 'row')
- root_solution: bfloat16 [8192, 256], P(('leaf', 'row'))
Inputs may be any that keep to these rules, and one draw needn't show every extreme that they name: `mid_rows_list`: each list of a child holds 2048 distinct rows of its middle supernode in increasing order, always with the first and the last. `root_rows_list`: each list of a child holds 2048 distinct rows of the root in increasing order, always with the first and the last. `mid_root_list`: each list holds 2048 distinct rows of the root in increasing order, always with the first and the last. `child_inverse`: lower triangular with a positive diagonal. `mid_inverse`: lower triangular with a positive diagonal. `root_inverse`: lower triangular with a positive diagonal.
All inputs are finite; a program needn't handle non-finite values.
Results may differ from a plain program's by a relative error of at most 0.0085.
Values may be sent and summed in bfloat16 or wider, within the bound.
A program may use at most 64 MiB of HBM per device.

v0:
```python
import jax
import jax.numpy as jnp
from jax import lax
from jax.sharding import PartitionSpec as P


def solve_spread(partial_value):
    placed = lax.psum(partial_value, "col").astype(jnp.bfloat16)
    whole_rows = lax.all_gather(placed, "row", axis=2, tiled=True)
    return (placed, whole_rows)


def gather_updates(pieces):
    return lax.all_gather(pieces, ("row", "col"), axis=2, tiled=True)


def scatter_block(values, rows_list, piece_rows, col_index):
    width = values.shape[-1]
    flat_values = values.reshape(-1, width).astype(jnp.float32)
    offsets = rows_list.reshape(-1) - col_index * piece_rows
    inside = (offsets >= 0) & (offsets < piece_rows)
    target = jnp.where(inside, offsets, piece_rows)
    summed = jnp.zeros((piece_rows + 1, width), jnp.float32).at[target].add(flat_values)
    return summed[:piece_rows]


def per_device(
    child_inverse,
    child_rhs,
    child_to_mid,
    child_to_root,
    mid_rows_list,
    root_rows_list,
    mid_inverse,
    mid_rhs,
    mid_to_root,
    mid_root_list,
    root_inverse,
    root_rhs,
):
    grid_size = lax.axis_size("row") * lax.axis_size("col")
    col_index = lax.axis_index("col")
    rhs_width = child_rhs.shape[3]
    child_partial = jnp.einsum(
        "gcij,gcjr->gcir", child_inverse, child_rhs, preferred_element_type=jnp.float32
    )
    child_local, child_whole = solve_spread(child_partial)
    mid_piece = child_to_mid.shape[2]
    root_piece = child_to_root.shape[2]
    update_mid = jnp.einsum(
        "gcuj,gcjr->gcur", child_to_mid, child_whole, preferred_element_type=jnp.float32
    ).astype(jnp.bfloat16)
    update_root = jnp.einsum(
        "gcuj,gcjr->gcur", child_to_root, child_whole, preferred_element_type=jnp.float32
    ).astype(jnp.bfloat16)
    stacked = jnp.concatenate((update_mid, update_root), axis=2)
    gathered = gather_updates(stacked)
    lead_count = gathered.shape[0]
    child_count = gathered.shape[1]
    split_view = gathered.reshape(
        lead_count, child_count, grid_size, mid_piece + root_piece, rhs_width
    )
    mid_updates = split_view[:, :, :, :mid_piece].reshape(
        lead_count, child_count, grid_size * mid_piece, rhs_width
    )
    root_updates = split_view[:, :, :, mid_piece:].reshape(
        lead_count, child_count, grid_size * root_piece, rhs_width
    )
    root_group = root_rhs.shape[0]
    child_root_term = scatter_block(root_updates, root_rows_list, root_group, col_index)
    mid_term = scatter_block(mid_updates, mid_rows_list, mid_rhs.shape[1], col_index)
    mid_input = (mid_rhs[0].astype(jnp.float32) - mid_term).astype(jnp.bfloat16)
    mid_partial = jnp.dot(mid_inverse[0], mid_input, preferred_element_type=jnp.float32)[None, None]
    mid_local, mid_whole = solve_spread(mid_partial)
    update_top = jnp.dot(
        mid_to_root[0], mid_whole[0, 0], preferred_element_type=jnp.float32
    ).astype(jnp.bfloat16)[None, None]
    top_whole = gather_updates(update_top)
    top_term = scatter_block(top_whole, mid_root_list, root_group, col_index)
    root_sum = lax.psum(child_root_term + top_term, "leaf")
    root_input = (root_rhs.astype(jnp.float32) - root_sum).astype(jnp.bfloat16)
    root_partial = jnp.dot(root_inverse, root_input, preferred_element_type=jnp.float32)
    root_solution = lax.psum(root_partial, "col").astype(jnp.bfloat16)
    return (child_local, mid_local[0], root_solution)


def solution(mesh):
    in_specs = (
        P("leaf", None, "row", "col"),
        P("leaf", None, "col", None),
        P("leaf", None, ("row", "col"), None),
        P("leaf", None, ("row", "col"), None),
        P("leaf", None, None),
        P("leaf", None, None),
        P("leaf", "row", "col"),
        P("leaf", "col", None),
        P("leaf", ("row", "col"), None),
        P("leaf", None),
        P(("leaf", "row"), "col"),
        P("col", None),
    )
    out_specs = (P("leaf", None, "row", None), P("leaf", "row", None), P(("leaf", "row"), None))
    return jax.shard_map(
        per_device, mesh=mesh, in_specs=in_specs, out_specs=out_specs, check_vma=False
    )
```

profile of v0, /device:TPU:8, one launch (start us, length us, event | category | flops | bytes accessed | tf_op | source)
XLA Modules:
  0.0 500.9 jit_solution(5121878186767649496)
XLA Ops:
  7.2 0.0 copy-start
  7.2 0.0 copy-start.5
  7.2 0.0 all-gather.6.cloned.1.call-start
  7.2 1.0 copy-done
  8.2 1.4 convolution_bitcast_fusion
  9.6 32.4 %all-reduce.6 = bf16[1,2,384,256]{3,2,1,0:T(8,128)(2,1)} all-reduce(f32[1,2,384,256]{3,2,1,0:T(8,128)S(1)} %convolution_bitcast_fusion), channel_id=1, replica_groups=mesh['leaf'=8,'row'=8,'col'=8] {'col'}, use_global_device_ids=true, to_apply=%region_0.0 | all-reduce | flops 196608 | bytes 1179648 | tf_op jit(solution)/shard_map/psum | solution.py:8
  42.0 0.0 copy-start.6
  42.0 0.0 all-gather.6.cloned.1.call-update
  42.0 0.0 all-gather.8.cloned.1.call-start
  42.1 49.2 %all-gather.6.cloned.1.call-done = bf16[1,2,3072,256]{3,2,1,0:T(8,128)(2,1)} async-done(((bf16[1,2,384,256]{3,2,1,0:T(8,128)(2,1)}), bf16[1,2,3072,256]{3,2,1,0:T(8,128)(2,1)}) %all-gather.6.cloned.1.call-update) | async-done | bytes 3145744 | tf_op jit(solution)/shard_map/all_gather | solution.py:9
  91.3 0.0 copy-done.5
  91.3 2.7 fusion.18
  94.0 0.0 copy-done.6
  94.0 0.1 copy-done.1
  94.1 0.6 fusion.21
  94.8 0.6 pad_maximum_fusion
  95.4 0.0 all-gather.8.cloned.1.call-update
  95.5 0.0 all-gather.10.cloned.1.call-start
  95.5 0.0 copy-done.8
  95.6 82.8 %all-gather.8.cloned.1.call-done = bf16[1,2,4096,256]{3,2,1,0:T(8,128)(2,1)} async-done(((bf16[1,2,64,256]{3,2,1,0:T(8,128)(2,1)}), bf16[1,2,4096,256]{3,2,1,0:T(8,128)(2,1)}) %all-gather.8.cloned.1.call-update) | async-done | bytes 4194320 | tf_op jit(solution)/shard_map/all_gather | solution.py:14
  178.4 4.2 fusion.42
  182.6 28.5 %scatter_custom_fusion = f32[513,256]{1,0:T(8,128)S(1)} fusion(s32[4096]{0:T(1024)S(1)} %bitcast.88, bf16[4096,256]{1,0:T(8,128)(2,1)} %bitcast.83, f32[]{:T(128)} %constant.7.clone.1), kind=kCustom, calls=%fused_computation.5 | custom fusion | flops 2097152 | bytes 2622468 | tf_op jit(solution)/shard_map/scatter-add | solution.py:23
  211.2 0.0 copy-done.7
  211.2 2.2 convolution_bitcast_fusion.1
  213.4 32.1 %all-reduce.7 = bf16[1,1,512,256]{2,3,1,0:T(8,128)(2,1)} all-reduce(f32[1,1,512,256]{2,3,1,0:T(8,128)} %convolution_bitcast_fusion.1), channel_id=1, replica_groups=mesh['leaf'=8,'row'=8,'col'=8] {'col'}, use_global_device_ids=true, to_apply=%region_2.3 | all-reduce | flops 131072 | bytes 786432 | tf_op jit(solution)/shard_map/psum | solution.py:8
  245.4 0.0 all-gather.10.cloned.1.call-update
  245.5 0.0 all-gather.12.cloned.1.call-start
  245.5 40.1 %all-gather.10.cloned.1.call-done = bf16[1,1,4096,256]{2,3,1,0:T(8,128)(2,1)} async-done(((bf16[1,1,512,256]{2,3,1,0:T(8,128)(2,1)}), bf16[1,1,4096,256]{2,3,1,0:T(8,128)(2,1)}) %all-gather.10.cloned.1.call-update) | async-done | bytes 2097168 | tf_op jit(solution)/shard_map/all_gather | solution.py:9
  285.7 2.9 fusion.27
  288.6 0.0 all-gather.12.cloned.1.call-update
  288.6 0.0 all-reduce.5.cloned.1.call-start
  288.7 0.0 copy-done.9
  288.7 0.0 copy-done.10
  288.8 29.2 %scatter_custom_fusion.1 = f32[1025,256]{1,0:T(8,128)} fusion(s32[4096]{0:T(1024)S(1)} %bitcast.89, bf16[4096,256]{1,0:T(8,128)(2,1)S(1)} %bitcast.82, f32[]{:T(128)} %constant.7.clone.1), kind=kCustom, calls=%fused_computation.3 | custom fusion | flops 2097152 | bytes 3146756 | tf_op jit(solution)/shard_map/scatter-add | solution.py:23
  318.0 51.5 %all-gather.12.cloned.1.call-done = bf16[2048,256]{1,0:T(8,128)(2,1)} async-done(((bf16[32,256]{1,0:T(8,128)(2,1)}), bf16[2048,256]{1,0:T(8,128)(2,1)}) %all-gather.12.cloned.1.call-update) | async-done | bytes 1048592 | tf_op jit(solution)/shard_map/all_gather | solution.py:14
  369.5 14.9 %scatter_custom_fusion.2 = f32[1025,256]{1,0:T(8,128)S(1)} fusion(s32[2048]{0:T(1024)S(1)} %bitcast.90, bf16[2048,256]{1,0:T(8,128)(2,1)} %all-gather.12.cloned.1.call-done, f32[]{:T(128)} %constant.7.clone.1), kind=kCustom, calls=%fused_computation.13 | custom fusion | flops 1048576 | bytes 2098180 | tf_op jit(solution)/shard_map/scatter-add | solution.py:23
  384.4 0.0 copy-done.2
  384.4 0.0 copy-start.3
  384.4 0.0 copy-start.4
  384.4 1.2 slice_add_fusion
  385.6 0.0 all-reduce.5.cloned.1.call-update
  385.6 0.0 copy-done.3
  385.6 0.8 copy.17
  386.5 80.8 %all-reduce.5.cloned.1.call-done = f32[1024,256]{1,0:T(8,128)} async-done(((f32[1024,256]{1,0:T(8,128)}), f32[1024,256]{1,0:T(8,128)}) %all-reduce.5.cloned.1.call-update) | async-done | bytes 1048592 | tf_op jit(solution)/shard_map/psum | solution.py:80
  467.3 0.0 copy-done.4
  467.3 1.6 convolution_bitcast_fusion.2
  468.9 24.7 %all-reduce.8 = bf16[128,256]{0,1:T(8,128)(2,1)S(1)} all-reduce(f32[128,256]{0,1:T(8,128)S(1)} %convolution_bitcast_fusion.2), channel_id=1, replica_groups=mesh['leaf'=8,'row'=8,'col'=8] {'col'}, use_global_device_ids=true, to_apply=%region_6.7 | all-reduce | flops 32768 | bytes 196608 | tf_op jit(solution)/shard_map/psum | solution.py:83
  493.6 0.7 copy.18
  (13 shorter events, 0.2 us)
Async XLA Ops:
  7.2 1.1 copy-start
  7.2 84.1 %copy-start.5 = (bf16[1,2,32,3072]{3,2,1,0:T(8,128)(2,1)S(1)}, bf16[1,2,32,3072]{3,2,1,0:T(8,128)(2,1)}, u32[]{:S(2)}) copy-start(bf16[1,2,32,3072]{3,2,1,0:T(8,128)(2,1)} %param.14) | copy-start | bytes 1179652
  7.2 84.1 %all-gather.6.cloned.1.call-start = ((), (), s32[]{:S(2)}) async-start(), calls=%async_computation | async-start | bytes 3538944 | tf_op jit(solution)/shard_map/all_gather | solution.py:9
  42.0 52.0 %copy-start.6 = (bf16[1,2,32,3072]{3,2,1,0:T(8,128)(2,1)S(1)}, bf16[1,2,32,3072]{3,2,1,0:T(8,128)(2,1)}, u32[]{:S(2)}) copy-start(bf16[1,2,32,3072]{3,2,1,0:T(8,128)(2,1)} %param.15) | copy-start | bytes 1179652
  42.0 136.4 %all-gather.8.cloned.1.call-start = ((), (), s32[]{:S(2)}) async-start(), calls=%async_computation.1 | async-start | bytes 4259840 | tf_op jit(solution)/shard_map/all_gather | solution.py:14
  91.3 2.8 copy-start.1
  94.1 1.4 copy-start.8
  95.5 190.2 %all-gather.10.cloned.1.call-start = ((), (), s32[]{:S(2)}) async-start(), calls=%async_computation.2 | async-start | bytes 2359296 | tf_op jit(solution)/shard_map/all_gather | solution.py:9
  182.6 28.5 %copy-start.7 = (bf16[1,512,256]{2,1,0:T(8,128)(2,1)S(1)}, bf16[1,512,256]{2,1,0:T(8,128)(2,1)}, u32[]{:S(2)}) copy-start(bf16[1,512,256]{2,1,0:T(8,128)(2,1)} %param.19) | copy-start | bytes 786436
  213.4 75.3 %copy-start.9 = (s32[1,2,2048]{2,1,0:T(2,128)S(1)}, s32[1,2,2048]{2,1,0:T(2,128)}, u32[]{:S(2)}) copy-start(s32[1,2,2048]{2,1,0:T(2,128)} %param.17) | copy-start | bytes 49156
  213.4 75.4 %copy-start.10 = (s32[1,2048]{1,0:T(1,128)S(1)}, s32[1,2048]{1,0:T(1,128)}, u32[]{:S(2)}) copy-start(s32[1,2048]{1,0:T(1,128)} %param.21) | copy-start | bytes 24580
  245.5 124.1 %all-gather.12.cloned.1.call-start = ((), (), s32[]{:S(2)}) async-start(), calls=%async_computation.4 | async-start | bytes 1064960 | tf_op jit(solution)/shard_map/all_gather | solution.py:14
  288.6 178.7 %all-reduce.5.cloned.1.call-start = ((), (), s32[]{:S(2)}) async-start(), calls=%async_computation.3 | async-start | bytes 2097152 | tf_op jit(solution)/shard_map/psum | solution.py:80
  318.0 66.4 %copy-start.2 = (f32[1025,256]{1,0:T(8,128)S(1)}, f32[1025,256]{1,0:T(8,128)}, u32[]{:S(2)}) copy-start(f32[1025,256]{1,0:T(8,128)} %scatter_custom_fusion.1) | copy-start | bytes 3148804
  384.4 1.2 copy-start.3
  384.4 82.9 %copy-start.4 = (bf16[1024,256]{1,0:T(8,128)(2,1)S(1)}, bf16[1024,256]{1,0:T(8,128)(2,1)}, u32[]{:S(2)}) copy-start(bf16[1024,256]{1,0:T(8,128)(2,1)} %param.23) | copy-start | bytes 1572868
Sparse Core Ops, SparseCore 0:
  42.2 49.0 all-gather.5
  95.6 82.8 all-gather.7
  245.6 40.0 all-gather.9
  289.4 80.0 all-gather.11
  385.8 81.4 all-reduce.4
where the time goes:
time: 501 us
  waiting for transfers between devices  305 us (61%)
  blocking collectives  89.2 us (18%)
  other arithmetic  74.5 us (15%)
  between operations  14 us (3%)
  matrix products  11.4 us (2%)
  local copies, waits for them, and re-layouts  7.04 us (1%)
    all_gather x2, waiting for transfers between devices, gather_updates(): return lax.all_gather(pieces, ('row', 'col'), axis=2, tiled=True)  134 us
    all_gather x2, waiting for transfers between devices, solve_spread(): whole_rows = lax.all_gather(placed, 'row', axis=2, tiled=True)  89.3 us
    psum x1, waiting for transfers between devices, per_device(): root_sum = lax.psum(child_root_term + top_term, 'leaf')  80.8 us
    scatter-add x3, other arithmetic, scatter_block(): jnp.zeros((piece_rows + 1, width), jnp.float32).at[target].add(flat_values)  72.6 us
    psum x2, blocking collectives, solve_spread(): placed = lax.psum(partial_value, 'col').astype(jnp.bfloat16)  64.5 us
    psum x1, blocking collectives, per_device(): root_solution = lax.psum(root_partial, 'col').astype(jnp.bfloat16)  24.7 us
  transfers between devices with their start and end apart: 5, of which 5 were waited for; matrix products, arithmetic and copies ran while one was open for 6% of the time, Pallas kernels for 0%

commit v1 on v0

--- a/solution.py
+++ b/solution.py
@@ -77,7 +77,7 @@
     ).astype(jnp.bfloat16)[None, None]
     top_whole = gather_updates(update_top)
     top_term = scatter_block(top_whole, mid_root_list, root_group, col_index)
-    root_sum = lax.psum(child_root_term + top_term, "leaf")
+    root_sum = jax.lax.all_gather(child_root_term + top_term, "leaf").sum(axis=0)
     root_input = (root_rhs.astype(jnp.float32) - root_sum).astype(jnp.bfloat16)
     root_partial = jnp.dot(root_inverse, root_input, preferred_element_type=jnp.float32)
     root_solution = lax.psum(root_partial, "col").astype(jnp.bfloat16)

time: 501 us -> 521 us (1.040)
  waiting for transfers between devices: 305 us -> 320 us
    all_gather x0 -> x1, waiting for transfers between devices: none -> 95.9 us  [per_device(): jax.lax.all_gather(child_root_term + top_term, 'leaf').sum(axis=0)]
    psum x1 -> x0, waiting for transfers between devices: 80.8 us -> none  [per_device(): root_sum = lax.psum(child_root_term + top_term, 'leaf')]
where the time goes in v1:
time: 521 us
  waiting for transfers between devices  320 us (61%)
  blocking collectives  91.1 us (17%)
  other arithmetic  78.6 us (15%)
  between operations  14 us (3%)
  matrix products  10.2 us (2%)
  local copies, waits for them, and re-layouts  7.05 us (1%)
    all_gather x2, waiting for transfers between devices, gather_updates(): return lax.all_gather(pieces, ('row', 'col'), axis=2, tiled=True)  134 us
    all_gather x1, waiting for transfers between devices, per_device(): jax.lax.all_gather(child_root_term + top_term, 'leaf').sum(axis=0)  95.9 us
    all_gather x2, waiting for transfers between devices, solve_spread(): whole_rows = lax.all_gather(placed, 'row', axis=2, tiled=True)  89.4 us
    scatter-add x3, other arithmetic, scatter_block(): jnp.zeros((piece_rows + 1, width), jnp.float32).at[target].add(flat_values)  72.6 us
    psum x2, blocking collectives, solve_spread(): placed = lax.psum(partial_value, 'col').astype(jnp.bfloat16)  64.5 us
    psum x1, blocking collectives, per_device(): root_solution = lax.psum(root_partial, 'col').astype(jnp.bfloat16)  26.6 us
  transfers between devices with their start and end apart: 5, of which 5 were waited for; matrix products, arithmetic and copies ran while one was open for 6% of the time, Pallas kernels for 0%

profile of v1, /device:TPU:8, one launch (start us, length us, event | category | flops | bytes accessed | tf_op | source)
XLA Modules:
  0.0 520.8 jit_solution(7180553577764983337)
XLA Ops:
  7.2 0.0 copy-start
  7.2 0.0 copy-start.5
  7.2 0.0 all-gather.8.cloned.1.call-start
  7.2 1.0 copy-done
  8.2 1.4 convolution_bitcast_fusion
  9.6 32.4 %all-reduce.3 = bf16[1,2,384,256]{3,2,1,0:T(8,128)(2,1)} all-reduce(f32[1,2,384,256]{3,2,1,0:T(8,128)S(1)} %convolution_bitcast_fusion), channel_id=1, replica_groups=mesh['leaf'=8,'row'=8,'col'=8] {'col'}, use_global_device_ids=true, to_apply=%region_0.0 | all-reduce | flops 196608 | bytes 1179648 | tf_op jit(solution)/shard_map/psum | solution.py:8
  42.0 0.0 all-gather.8.cloned.1.call-update
  42.0 0.0 all-gather.10.cloned.1.call-start
  42.1 49.2 %all-gather.8.cloned.1.call-done = bf16[1,2,3072,256]{3,2,1,0:T(8,128)(2,1)} async-done(((bf16[1,2,384,256]{3,2,1,0:T(8,128)(2,1)}), bf16[1,2,3072,256]{3,2,1,0:T(8,128)(2,1)}) %all-gather.8.cloned.1.call-update) | async-done | bytes 3145744 | tf_op jit(solution)/shard_map/all_gather | solution.py:9
  91.3 0.0 copy-done.5
  91.3 2.7 fusion.21
  94.0 0.0 copy-done.6
  94.0 0.1 copy-done.1
  94.1 0.6 fusion.18
  94.8 0.6 pad_maximum_fusion
  95.4 0.0 all-gather.10.cloned.1.call-update
  95.5 0.0 all-gather.12.cloned.1.call-start
  95.5 0.0 copy-done.9
  95.6 82.8 %all-gather.10.cloned.1.call-done = bf16[1,2,4096,256]{3,2,1,0:T(8,128)(2,1)} async-done(((bf16[1,2,64,256]{3,2,1,0:T(8,128)(2,1)}), bf16[1,2,4096,256]{3,2,1,0:T(8,128)(2,1)}) %all-gather.10.cloned.1.call-update) | async-done | bytes 4194320 | tf_op jit(solution)/shard_map/all_gather | solution.py:14
  178.4 4.2 fusion.42
  182.7 28.5 %scatter_custom_fusion = f32[513,256]{1,0:T(8,128)S(1)} fusion(s32[4096]{0:T(1024)S(1)} %bitcast.90, bf16[4096,256]{1,0:T(8,128)(2,1)} %bitcast.85, f32[]{:T(128)} %constant.7.clone.1), kind=kCustom, calls=%fused_computation.5 | custom fusion | flops 2097152 | bytes 2622468 | tf_op jit(solution)/shard_map/scatter-add | solution.py:23
  211.2 0.0 copy-done.7
  211.2 2.2 convolution_bitcast_fusion.1
  213.4 32.1 %all-reduce.4 = bf16[1,1,512,256]{2,3,1,0:T(8,128)(2,1)} all-reduce(f32[1,1,512,256]{2,3,1,0:T(8,128)} %convolution_bitcast_fusion.1), channel_id=1, replica_groups=mesh['leaf'=8,'row'=8,'col'=8] {'col'}, use_global_device_ids=true, to_apply=%region_2.3 | all-reduce | flops 131072 | bytes 786432 | tf_op jit(solution)/shard_map/psum | solution.py:8
  245.5 0.0 all-gather.12.cloned.1.call-update
  245.5 0.0 all-gather.14.cloned.1.call-start
  245.5 40.1 %all-gather.12.cloned.1.call-done = bf16[1,1,4096,256]{2,3,1,0:T(8,128)(2,1)} async-done(((bf16[1,1,512,256]{2,3,1,0:T(8,128)(2,1)}), bf16[1,1,4096,256]{2,3,1,0:T(8,128)(2,1)}) %all-gather.12.cloned.1.call-update) | async-done | bytes 2097168 | tf_op jit(solution)/shard_map/all_gather | solution.py:9
  285.7 2.9 fusion.27
  288.6 0.0 all-gather.14.cloned.1.call-update
  288.6 0.0 all-gather.16.cloned.1.call-start
  288.7 0.0 copy-done.10
  288.7 0.0 copy-done.11
  288.8 29.2 %scatter_custom_fusion.1 = f32[1025,256]{1,0:T(8,128)} fusion(s32[4096]{0:T(1024)S(1)} %bitcast.91, bf16[4096,256]{1,0:T(8,128)(2,1)S(1)} %bitcast.84, f32[]{:T(128)} %constant.7.clone.1), kind=kCustom, calls=%fused_computation.3 | custom fusion | flops 2097152 | bytes 3146756 | tf_op jit(solution)/shard_map/scatter-add | solution.py:23
  318.0 51.5 %all-gather.14.cloned.1.call-done = bf16[2048,256]{1,0:T(8,128)(2,1)} async-done(((bf16[32,256]{1,0:T(8,128)(2,1)}), bf16[2048,256]{1,0:T(8,128)(2,1)}) %all-gather.14.cloned.1.call-update) | async-done | bytes 1048592 | tf_op jit(solution)/shard_map/all_gather | solution.py:14
  369.6 14.9 %scatter_custom_fusion.2 = f32[1025,256]{1,0:T(8,128)S(1)} fusion(s32[2048]{0:T(1024)S(1)} %bitcast.92, bf16[2048,256]{1,0:T(8,128)(2,1)} %all-gather.14.cloned.1.call-done, f32[]{:T(128)} %constant.7.clone.1), kind=kCustom, calls=%fused_computation.13 | custom fusion | flops 1048576 | bytes 2098180 | tf_op jit(solution)/shard_map/scatter-add | solution.py:23
  384.4 0.0 copy-done.2
  384.4 0.0 copy-start.3
  384.4 1.2 slice_add_fusion
  385.6 0.0 all-gather.16.cloned.1.call-update
  385.6 0.0 copy-done.3
  385.7 0.8 copy.17
  386.5 95.9 %all-gather.16.cloned.1.call-done = f32[8192,256]{1,0:T(8,128)} async-done(((f32[1024,256]{1,0:T(8,128)}), f32[8192,256]{1,0:T(8,128)}) %all-gather.16.cloned.1.call-update) | async-done | bytes 8388624 | tf_op jit(solution)/shard_map/all_gather | solution.py:80
  482.4 4.1 reduce_sum.9
  486.5 0.0 copy-done.4
  486.5 0.0 copy-done.8
  486.5 0.4 convolution_bitcast_fusion.2
  486.9 26.6 %all-reduce.5 = bf16[128,256]{0,1:T(8,128)(2,1)S(1)} all-reduce(f32[128,256]{0,1:T(8,128)S(1)} %convolution_bitcast_fusion.2), channel_id=1, replica_groups=mesh['leaf'=8,'row'=8,'col'=8] {'col'}, use_global_device_ids=true, to_apply=%region_6.7 | all-reduce | flops 32768 | bytes 196608 | tf_op jit(solution)/shard_map/psum | solution.py:83
  513.5 0.7 copy.18
  (16 shorter events, 0.2 us)
Async XLA Ops:
  7.2 1.1 copy-start
  7.2 84.1 %copy-start.5 = (bf16[1,2,32,3072]{3,2,1,0:T(8,128)(2,1)S(1)}, bf16[1,2,32,3072]{3,2,1,0:T(8,128)(2,1)}, u32[]{:S(2)}) copy-start(bf16[1,2,32,3072]{3,2,1,0:T(8,128)(2,1)} %param.15) | copy-start | bytes 1179652
  7.2 84.1 %all-gather.8.cloned.1.call-start = ((), (), s32[]{:S(2)}) async-start(), calls=%async_computation | async-start | bytes 3538944 | tf_op jit(solution)/shard_map/all_gather | solution.py:9
  42.0 52.0 %copy-start.6 = (bf16[1,2,32,3072]{3,2,1,0:T(8,128)(2,1)S(1)}, bf16[1,2,32,3072]{3,2,1,0:T(8,128)(2,1)}, u32[]{:S(2)}) copy-start(bf16[1,2,32,3072]{3,2,1,0:T(8,128)(2,1)} %param.14) | copy-start | bytes 1179652
  42.0 136.4 %all-gather.10.cloned.1.call-start = ((), (), s32[]{:S(2)}) async-start(), calls=%async_computation.1 | async-start | bytes 4259840 | tf_op jit(solution)/shard_map/all_gather | solution.py:14
  91.3 2.8 copy-start.1
  94.1 1.4 copy-start.9
  95.5 190.2 %all-gather.12.cloned.1.call-start = ((), (), s32[]{:S(2)}) async-start(), calls=%async_computation.2 | async-start | bytes 2359296 | tf_op jit(solution)/shard_map/all_gather | solution.py:9
  182.7 28.5 %copy-start.7 = (bf16[1,512,256]{2,1,0:T(8,128)(2,1)S(1)}, bf16[1,512,256]{2,1,0:T(8,128)(2,1)}, u32[]{:S(2)}) copy-start(bf16[1,512,256]{2,1,0:T(8,128)(2,1)} %param.19) | copy-start | bytes 786436
  213.4 75.3 %copy-start.10 = (s32[1,2,2048]{2,1,0:T(2,128)S(1)}, s32[1,2,2048]{2,1,0:T(2,128)}, u32[]{:S(2)}) copy-start(s32[1,2,2048]{2,1,0:T(2,128)} %param.17) | copy-start | bytes 49156
  213.4 75.4 %copy-start.11 = (s32[1,2048]{1,0:T(1,128)S(1)}, s32[1,2048]{1,0:T(1,128)}, u32[]{:S(2)}) copy-start(s32[1,2048]{1,0:T(1,128)} %param.21) | copy-start | bytes 24580
  245.5 124.1 %all-gather.14.cloned.1.call-start = ((), (), s32[]{:S(2)}) async-start(), calls=%async_computation.3 | async-start | bytes 1064960 | tf_op jit(solution)/shard_map/all_gather | solution.py:14
  288.6 193.7 %all-gather.16.cloned.1.call-start = ((), (), s32[]{:S(2)}) async-start(), calls=%async_computation.4 | async-start | bytes 9437184 | tf_op jit(solution)/shard_map/all_gather | solution.py:80
  318.0 66.4 %copy-start.2 = (f32[1025,256]{1,0:T(8,128)S(1)}, f32[1025,256]{1,0:T(8,128)}, u32[]{:S(2)}) copy-start(f32[1025,256]{1,0:T(8,128)} %scatter_custom_fusion.1) | copy-start | bytes 3148804
  384.4 1.2 copy-start.3
  482.4 4.1 copy-start.4
  482.4 4.1 copy-start.8
Sparse Core Ops, SparseCore 0:
  42.2 49.0 all-gather.7
  95.6 82.8 all-gather.9
  245.6 40.0 all-gather.11
  289.4 80.0 all-gather.13
  385.8 96.5 all-gather.15
